TPU v7x, 256 devices: a whole 4x4x8 slice. The times are simulated.
256 devices in a mesh: req: 32 (over z_lo, x, core), tp: 8 (over z_hi, y).
Axes of the slice: x: 4, y: 4, z: 8 (z_hi: 2, z_lo: 4; z = z_hi * 4 + z_lo), core: 2. Of those that a mesh axis runs over, the one named last changes fastest.
Arguments:
- hidden: bfloat16 [8192, 4608], P('req', 'tp'), may hold values from -6 to 6
- norm_gain: float32 [4608], replicated, may hold values from 0.1 to 1.9
- w_query: bfloat16 [4608, 4096], P(None, 'tp'), may hold values from -0.25 to 0.25
- w_key: bfloat16 [4608, 2048], P(None, 'tp'), may hold values from -0.09375 to 0.09375
- w_value: bfloat16 [4608, 2048], P(None, 'tp'), may hold values from -0.09375 to 0.09375
- prefix_kv: bfloat16 [16384, 2, 2048], P('req', None, 'tp'), may hold values from -6 to 6
- group_of: int32 [32], replicated, may hold values from 0 to 3, as said below
- block_owner: int32 [4, 8], replicated, may hold values from 0 to 31, as said below
- lengths: int32 [32], replicated, may hold values from 32 to 256, as said below
Outputs:
- attended: bfloat16 [8192, 4096], P('req', 'tp')
- key_cache: bfloat16 [8192, 2048], P('req', 'tp')
- value_cache: bfloat16 [8192, 2048], P('req', 'tp')
Inputs may be any that keep to these rules, and one draw needn't show every extreme that they name: `group_of`: every group holds exactly 8 requests. `block_owner`: every block index appears exactly once. `lengths`: some request has exactly 256 live rows and some exactly 32.
All inputs are finite; a program needn't handle non-finite values.
Results may differ from a plain program's by a relative error of at most 0.011.
Values may be sent and summed in bfloat16 or wider, within the bound.
A program may use at most 256 MiB of HBM per device.

v0:
```python
import math

import jax
import jax.numpy as jnp
from jax import lax
from jax.sharding import PartitionSpec as P

HD = 128
GSIZE = 8
PREFIX = 4096


SOFTCAP = 50.0
EPSILON = 1e-06
QUERY_SCALE = 1.0 / 12.0


def rope_tables(positions, head_width):
    half_width = head_width // 2
    inverse_freq = jnp.exp(
        jnp.arange(half_width).astype(jnp.float32) * (-2.0 * math.log(10000.0) / head_width)
    )
    angles = positions.astype(jnp.float32)[:, None] * inverse_freq[None, :]
    return (jnp.cos(angles), jnp.sin(angles))


def rotate(values, cosine_table, sine_table):
    half_width = values.shape[-1] // 2
    lower_half = values[..., :half_width]
    upper_half = values[..., half_width:]
    cosine_part = cosine_table[:, None, :]
    sine_part = sine_table[:, None, :]
    return jnp.concatenate(
        [
            lower_half * cosine_part - upper_half * sine_part,
            upper_half * cosine_part + lower_half * sine_part,
        ],
        axis=-1,
    )


def attend(grouped, key_block, value_block, allowed_mask):
    scores = jnp.einsum("rkgd,ckd->kgrc", grouped, key_block, preferred_element_type=jnp.float32)
    weights = jnp.exp(SOFTCAP * jnp.tanh(scores / SOFTCAP))
    if allowed_mask is not None:
        weights = jnp.where(allowed_mask[None, None], weights, 0.0)
    denominator = jnp.transpose(jnp.sum(weights, axis=3), (2, 0, 1))
    numerator = jnp.einsum(
        "kgrc,ckd->rkgd",
        weights.astype(jnp.bfloat16),
        value_block,
        preferred_element_type=jnp.float32,
    )
    return (numerator, denominator)


def body(hidden, norm_gain, w_query, w_key, w_value, prefix_kv, group_of, block_owner, lengths):
    device = lax.axis_index("req")
    row_count = hidden.shape[0]
    gathered = lax.all_gather(hidden, "tp", axis=1, tiled=True)
    features = gathered.astype(jnp.float32)
    row_scale = lax.rsqrt(jnp.mean(features * features, axis=1, keepdims=True) + EPSILON)
    normed = (features * row_scale * norm_gain[None, :]).astype(jnp.bfloat16)
    heads_query = w_query.shape[1] // HD
    heads_kv = w_key.shape[1] // HD
    group_size = heads_query // heads_kv
    query_raw = jnp.dot(normed, w_query, preferred_element_type=jnp.float32)
    key_raw = jnp.dot(normed, w_key, preferred_element_type=jnp.float32)
    value_raw = jnp.dot(normed, w_value, preferred_element_type=jnp.float32)
    cosine_table, sine_table = rope_tables(jnp.arange(row_count) + PREFIX, HD)
    query_rows = (
        rotate(query_raw.reshape(row_count, heads_query, HD), cosine_table, sine_table)
        * QUERY_SCALE
    ).astype(jnp.bfloat16)
    live_rows = jnp.arange(row_count) < lengths[device]
    key_rows = jnp.where(
        live_rows[:, None, None],
        rotate(key_raw.reshape(row_count, heads_kv, HD), cosine_table, sine_table),
        0.0,
    ).astype(jnp.bfloat16)
    value_rows = jnp.where(live_rows[:, None], value_raw, 0.0).astype(jnp.bfloat16)
    grouped = query_rows.reshape(row_count, heads_kv, group_size, HD)
    causal = jnp.arange(row_count)[:, None] >= jnp.arange(row_count)[None, :]
    numerator, denominator = attend(
        grouped, key_rows, value_rows.reshape(row_count, heads_kv, HD), causal
    )
    device_count = lax.axis_size("req")
    flat_query = query_rows.reshape(row_count, heads_query * HD)
    everyone = lax.all_gather(flat_query, "req", axis=0, tiled=True)
    owned_group = jnp.sum(
        jnp.any(block_owner == device, axis=1).astype(jnp.int32)
        * jnp.arange(block_owner.shape[0], dtype=jnp.int32)
    )
    members = jnp.argsort((group_of != owned_group).astype(jnp.int32), stable=True)[:GSIZE]
    chosen = everyone.reshape(device_count, row_count, heads_kv, group_size, HD)[members]
    block_count = prefix_kv.shape[0]
    key_block = prefix_kv[:, 0].reshape(block_count, heads_kv, HD)
    value_block = prefix_kv[:, 1].reshape(block_count, heads_kv, HD)
    extra_num, extra_den = attend(
        chosen.reshape(GSIZE * row_count, heads_kv, group_size, HD), key_block, value_block, None
    )
    full_num = jnp.zeros((device_count, row_count, heads_kv * group_size * HD), jnp.float32)
    full_num = full_num.at[members].set(
        extra_num.reshape(GSIZE, row_count, heads_kv * group_size * HD)
    )
    full_den = jnp.zeros((device_count, row_count, heads_kv * group_size), jnp.float32)
    full_den = full_den.at[members].set(extra_den.reshape(GSIZE, row_count, heads_kv * group_size))
    got_num, got_den = (
        lax.psum_scatter(
            full_num.reshape(device_count * row_count, -1), "req", scatter_dimension=0, tiled=True
        ),
        lax.psum_scatter(
            full_den.reshape(device_count * row_count, -1), "req", scatter_dimension=0, tiled=True
        ),
    )
    numerator = numerator + got_num.reshape(numerator.shape)
    denominator = denominator + got_den.reshape(denominator.shape)
    attended = numerator / denominator[..., None]
    attended = jnp.where(live_rows[:, None, None, None], attended, 0.0).astype(jnp.bfloat16)
    return (
        attended.reshape(row_count, heads_query * HD),
        key_rows.reshape(row_count, heads_kv * HD),
        value_rows,
    )


def solution(mesh):
    in_specs = (
        P("req", "tp"),
        P(),
        P(None, "tp"),
        P(None, "tp"),
        P(None, "tp"),
        P("req", None, "tp"),
        P(),
        P(),
        P(),
    )
    out_specs = (P("req", "tp"), P("req", "tp"), P("req", "tp"))
    return jax.shard_map(body, mesh=mesh, in_specs=in_specs, out_specs=out_specs, check_vma=False)
```

profile of v0, /device:TPU:1, one launch (start us, length us, event | category | flops | bytes accessed | tf_op | source)
XLA Modules:
  0.0 562.2 jit_solution(6024013331039307176)
XLA Ops:
  7.2 0.7 all-gather.3.cloned.1.call-update
  8.0 1.2 multiply_cosine_fusion
  9.2 83.8 %all-gather.3.cloned.1.call-done = bf16[256,4608]{0,1:T(8,128)(2,1)} async-done(((bf16[256,576]{0,1:T(8,128)(2,1)}), bf16[256,4608]{0,1:T(8,128)(2,1)}) %all-gather.3.cloned.1.call-update) | async-done | bytes 2359312 | tf_op jit(solution)/shard_map/all_gather | solution.py:60
  92.9 2.3 fusion.1
  95.2 5.6 fusion.30
  100.9 1.0 copy.140
  101.9 1.0 copy.139
  102.9 1.3 multiply_subtract_fusion
  104.3 0.8 copy-done.2
  105.1 0.9 fusion.16
  106.0 1.8 copy.106
  108.1 1.8 fusion.35
  109.9 1.9 copy.141
  111.7 1.2 copy.142
  113.8 0.6 compare_convert_fusion
  114.4 1.6 sort.17
  116.1 76.1 %all-gather.5.cloned.1.call-done = bf16[8192,512]{0,1:T(8,128)(2,1)} async-done(((bf16[256,512]{0,1:T(8,128)(2,1)}), bf16[8192,512]{0,1:T(8,128)(2,1)}) %all-gather.5.cloned.1.call-update) | async-done | bytes 8388624 | tf_op jit(solution)/shard_map/all_gather | solution.py:89
  192.2 9.5 %copy.143 = bf16[64,8,32,256]{3,2,1,0:T(8,128)(2,1)} copy(bf16[64,8,32,256]{3,1,2,0:T(8,128)(2,1)} %bitcast.85) | data formatting | bytes 16777216
  201.7 14.6 %copy.107 = bf16[32,256,2,2,128]{4,1,3,2,0:T(8,128)(2,1)} copy(bf16[32,256,2,2,128]{1,0,4,3,2:T(8,128)(2,1)} %bitcast.83) | data formatting | bytes 16777216 | tf_op jit(solution)/shard_map/reshape | solution.py:95
  216.3 5.6 gather_fusion
  221.9 1.8 copy.108
  223.7 9.2 %bitcast_reduce_fusion = (f32[2,2,2048]{2,1,0:T(2,128)S(1)}, f32[2,2048,2,512]{1,3,2,0:T(8,128)}) fusion(bf16[2048,2,2,128]{3,0,2,1:T(8,128)(2,1)S(1)} %bitcast.86, bf16[512,2,128,1]{0,2,3,1:T(8,128)(2,1)} %bitcast.92), kind=kOutput, calls=%fused_computation.3 | convolution fusion | flops 1086316544 | bytes 19169280 | tf_op jit(solution)/shard_map/rkgd,ckd->kgrc/dot_general | solution.py:43
  232.9 0.7 scatter_fusion.1
  233.7 2.7 copy.134
  236.7 13.0 %fusion.4 = f32[2048,2,2,128]{3,0,2,1:T(8,128)} fusion(bf16[512,2,128,1]{0,2,3,1:T(8,128)(2,1)S(1)} %bitcast.90, f32[2,2048,2,512]{1,3,2,0:T(8,128)} %get-tuple-element.36), kind=kOutput, calls=%fused_computation.12 | convolution fusion | flops 1086324736 | bytes 21233664 | tf_op jit(solution)/shard_map/kgrc,ckd->rkgd/dot_general | solution.py:48
  249.7 8.7 %copy.133 = f32[2048,2,2,128]{3,2,1,0:T(2,128)} copy(f32[2048,2,2,128]{3,0,2,1:T(8,128)} %fusion.4) | data formatting | bytes 8388608 | tf_op jit(solution)/shard_map/reshape | solution.py:104
  258.4 6.4 %reshape.187 = f32[8,256,512]{2,1,0:T(8,128)} reshape(f32[2048,2,2,128]{3,2,1,0:T(2,128)} %copy.133) | data formatting | bytes 8388608 | tf_op jit(solution)/shard_map/reshape | solution.py:104
  264.8 7.9 %broadcast_in_dim.81 = f32[32,256,512]{2,1,0:T(8,128)} broadcast(f32[]{:T(128)} %constant.6.clone.1), dimensions={} | broadcast | bytes 16777220 | tf_op jit(solution)/shard_map/broadcast_in_dim | solution.py:102
  272.7 8.1 %scatter_fusion = f32[32,256,512]{2,1,0:T(8,128)} fusion(f32[32,256,512]{2,1,0:T(8,128)} %broadcast_in_dim.81, s32[8]{0:T(128)S(1)} %compare_select_fusion, f32[8,256,512]{2,1,0:T(8,128)} %reshape.187), kind=kCustom, calls=%fused_computation.1 | custom fusion | bytes 12582944 | tf_op jit(solution)/shard_map/scatter | solution.py:103
  280.8 17.5 %copy.116 = f32[8192,512]{0,1:T(8,128)} copy(f32[8192,512]{1,0:T(8,128)} %bitcast.82) | data formatting | bytes 33554432 | tf_op jit(solution)/shard_map/reshape | solution.py:110
  299.5 0.6 iota_compare_fusion.1
  300.2 0.6 iota_compare_fusion
  300.8 3.2 fusion.14
  304.6 0.8 copy.121
  305.4 4.0 fusion.32
  309.4 0.7 fusion.37
  310.1 1.7 copy.138
  311.8 1.7 copy.137
  313.6 1.1 multiply_subtract_fusion.1
  314.8 0.8 copy.118
  315.6 1.6 fusion.19
  317.2 1.7 copy.120
  318.9 2.3 fusion.38
  321.1 61.4 %reduce-scatter.7.cloned.1.call-done = f32[256,4]{1,0:T(8,128)} async-done(((f32[8192,4]{1,0:T(8,128)}), f32[256,4]{1,0:T(8,128)}) %reduce-scatter.7.cloned.1.call-update) | async-done | bytes 4112
  382.5 1.0 copy.135
  383.5 169.8 %reduce-scatter.5.cloned.1.call-done = f32[256,512]{0,1:T(8,128)} async-done(((f32[8192,512]{0,1:T(8,128)}), f32[256,512]{0,1:T(8,128)}) %reduce-scatter.5.cloned.1.call-update) | async-done | bytes 524304 | tf_op jit(solution)/shard_map/reduce_scatter | solution.py:109
  553.3 1.5 fusion.13
  554.8 0.8 copy.119
  (40 shorter events, 3.5 us)
Async XLA Ops:
  7.2 293.6 %copy-start = (bf16[4608,256]{1,0:T(8,128)(2,1)S(1)}, bf16[4608,256]{1,0:T(8,128)(2,1)}, u32[]{:S(2)}) copy-start(bf16[4608,256]{1,0:T(8,128)(2,1)} %param.13) | copy-start | bytes 7077892
  7.2 85.8 %all-gather.3.cloned.1.call-start = ((), (), s32[]{:S(2)}) async-start(), calls=%async_computation.2 | async-start | bytes 2654208 | tf_op jit(solution)/shard_map/all_gather | solution.py:60
  7.9 184.3 %all-gather.5.cloned.1.call-start = ((), (), s32[]{:S(2)}) async-start(), calls=%async_computation.3 | async-start | bytes 8650752 | tf_op jit(solution)/shard_map/all_gather | solution.py:89
  100.8 7.2 %copy-start.1 = (bf16[512,2,256]{2,1,0:T(2,128)(2,1)S(1)}, bf16[512,2,256]{2,1,0:T(2,128)(2,1)}, u32[]{:S(2)}) copy-start(bf16[512,2,256]{2,1,0:T(2,128)(2,1)} %param.14) | copy-start | bytes 1572868
  100.9 12.1 %copy-start.5 = (s32[4,8]{1,0:T(4,128)S(1)}, s32[4,8]{1,0:T(4,128)}, u32[]{:S(2)}) copy-start(s32[4,8]{1,0:T(4,128)} %param.16) | copy-start | bytes 388
  100.9 12.9 %copy-start.7 = (s32[32]{0:T(128)S(1)}, s32[32]{0:T(128)}, u32[]{:S(2)}) copy-start(s32[32]{0:T(128)} %param.15) | copy-start | bytes 388
  104.3 0.8 copy-start.2
  107.8 274.7 %reduce-scatter.7.cloned.1.call-start = ((), (), s32[]{:S(2)}) async-start(), calls=%async_computation.5 | async-start | bytes 4325376
  236.4 316.9 %reduce-scatter.5.cloned.1.call-start = ((), (), s32[]{:S(2)}) async-start(), calls=%async_computation.4 | async-start | bytes 17301504 | tf_op jit(solution)/shard_map/reduce_scatter | solution.py:109
  298.3 0.7 copy-start.8
  298.3 2.5 copy-start.6
  304.0 0.6 copy-start.4
  305.4 13.4 %copy-start.3 = (f32[256,4,64]{2,0,1:T(8,128)S(1)}, f32[256,4,64]{2,0,1:T(8,128)}, u32[]{:S(2)}) copy-start(f32[256,4,64]{2,0,1:T(8,128)} %copy-done.2) | copy-start | bytes 786436
Sparse Core Ops, SparseCore 0:
  10.6 82.2 all-gather.2
  107.9 84.1 all-gather.4
  236.5 145.9 reduce-scatter.6
  384.9 168.3 reduce-scatter.4
where the time goes:
time: 568 us; the launch traced here: 562 us
  waiting for transfers between devices  392 us (69%)
  local copies, waits for them, and re-layouts  104 us (18%)
  matrix products  38.6 us (7%)
  between operations  14 us (2%)
  other arithmetic  12.9 us (2%)
    reduce_scatter x1, waiting for transfers between devices, body(): lax.psum_scatter(full_num.reshape(device_count * row_count, -1), 'req', s...  170 us
    all_gather x1, waiting for transfers between devices, body(): gathered = lax.all_gather(hidden, 'tp', axis=1, tiled=True)  83.8 us
    all_gather x1, waiting for transfers between devices, body(): everyone = lax.all_gather(flat_query, 'req', axis=0, tiled=True)  76.1 us
    unnamed x5, waiting for transfers between devices  62.1 us
    unnamed x30, local copies, waits for them, and re-layouts  27.2 us
    reshape x1, local copies, waits for them, and re-layouts, body(): full_num.reshape(device_count * row_count, -1)  17.5 us
    reshape x2, local copies, waits for them, and re-layouts, body(): extra_num.reshape(GSIZE, row_count, heads_kv * group_size * HD)  15.2 us
    reshape x1, local copies, waits for them, and re-layouts, body(): everyone.reshape(device_count, row_count, heads_kv, group_size, HD)[members]  14.6 us
  transfers between devices with their start and end apart: 4, of which 4 were waited for; matrix products, arithmetic and copies ran while one was open for 17% of the time, Pallas kernels for 0%

commit v1 on v0

v1 whole, which is shorter than its diff:
```python
import functools
import math

import jax
import jax.numpy as jnp
import numpy as np
from jax import lax
from jax.experimental import pallas as pl
from jax.experimental.pallas import tpu as pltpu
from jax.sharding import PartitionSpec as P

MESH = pl.DeviceIdType.MESH
BF = jnp.bfloat16
F32 = jnp.float32
HD = 128
ROWS = 256
PREFIX = 4096
FEAT = 576
TP = 8
SL = 64
LOG2E = 1.4426950408889634


def rope_constants():
    freq = np.exp(np.arange(64, dtype=np.float32) * np.float32(-2.0 * math.log(10000.0) / 128))
    angle = (np.arange(ROWS) + PREFIX).astype(np.float32)[:, None] * freq[None, :]
    cosine, sine = np.cos(angle.astype(np.float64)), np.sin(angle.astype(np.float64))
    full_cos = np.concatenate([cosine, cosine], axis=1).astype(np.float32)
    signed_sin = np.concatenate([-sine, sine], axis=1).astype(np.float32)
    return full_cos, signed_sin


def kernel(
    group_ref, owner_ref, length_ref, hid, wq, wk, wv, kv, gain_ref, cos_ref, sin_ref,
    att_ref, key_ref, val_ref,
    hbuf, wbuf, kvb0, kvb1, qb0, qb1, ns0, ns1, nr0, nr1, ds0, ds1, dr0, dr1,
    acc, sq, gcol, kscr, vscr, snum, sden,
    lsem, wsem, qss, qsr, hs, hr, cs, cr, zs, zr, qs, qr, rs, rr, es, er,
):
    kvb, qb, ns, nr, ds, dr = (kvb0, kvb1), (qb0, qb1), (ns0, ns1), (nr0, nr1), (ds0, ds1), (dr0, dr1)
    me = lax.axis_index("req")
    t = lax.axis_index("tp")
    p, s = me // 8, me % 8
    c = s % 2
    zh, y = t // 4, t % 4
    inner = (p * (3 - p)) // 2
    mid = inner == 1
    zo = (p + 1 - 2 * (p % 2), 2 - p // 2, 3 - 3 * (p // 2))

    def row_dev(slot):
        return (p * 8 + slot, t)

    def z_dev(z):
        return (z * 8 + s, t)

    def tp_dev(other):
        return (me, other)

    def slot_at(rel):
        return (s + rel) % 8

    def copy_to(src, dst, send, recv, dev):
        return pltpu.make_async_remote_copy(src, dst, send, recv, device_id=dev, device_id_type=MESH)

    sibling = p * 8 + s + 1 - 2 * c
    partner = (1 - zh) * 4 + y
    ys = [(y + 1) % 4, (y + 3) % 4, (y + 2) % 4]
    yin = [(y + 3) % 4, (y + 1) % 4, (y + 2) % 4]

    own_hid = pltpu.make_async_copy(hid, hbuf.at[t], lsem.at[0])
    own_hid.start()
    own_kv = [
        pltpu.make_async_copy(kv.at[h, pl.ds(s * SL, SL)], kvb[h].at[me], lsem.at[1 + h])
        for h in range(2)
    ]
    loads = [
        pltpu.make_async_copy(wq, wbuf.at[:, 0:512], wsem.at[0]),
        pltpu.make_async_copy(wk, wbuf.at[:, 512:768], wsem.at[1]),
        pltpu.make_async_copy(wv, wbuf.at[:, 768:1024], wsem.at[2]),
    ]

    barrier = pltpu.get_barrier_semaphore()
    greet = [row_dev(slot_at(rel)) for rel in range(1, 8)]
    greet += [z_dev(zo[0])] + [tp_dev((t + i) % TP) for i in range(1, TP)]
    for dev in greet:
        pl.semaphore_signal(barrier, inc=1, device_id=dev, device_id_type=MESH)

    @pl.when(mid)
    def _():
        pl.semaphore_signal(barrier, inc=1, device_id=z_dev(3 - p), device_id_type=MESH)

    eye = lax.broadcasted_iota(jnp.int32, (HD, HD), 0) == lax.broadcasted_iota(jnp.int32, (HD, HD), 1)
    own_hid.wait()
    features = hbuf[t].astype(F32)
    sq[t] = jnp.broadcast_to(jnp.sum(features * features, axis=0, keepdims=True), (8, ROWS))
    pl.semaphore_wait(barrier, len(greet) + inner)

    pending = []

    def go(copy):
        copy.start()
        pending.append(copy)

    def sq_copy(i):
        return copy_to(sq.at[t], sq.at[t], qss.at[i], qsr.at[i], tp_dev((t + i) % TP))

    def sq_wait(i):
        ref = sq.at[(t + TP - i) % TP]
        copy_to(ref, ref, qss.at[i], qsr.at[i], tp_dev(t)).wait_recv()

    for i in range(1, TP):
        go(sq_copy(i))

    def hid_copy(i, src, holder, dev):
        return copy_to(src, hbuf.at[holder], hs.at[i], hr.at[i], tp_dev(dev))

    go(hid_copy(0, hid, t, partner))
    for i, o in enumerate(ys):
        go(hid_copy(1 + i, hid, t, zh * 4 + o))

    def scatter(h, rel):
        slot = slot_at(rel)
        src = kv.at[h, pl.ds(pl.multiple_of(slot * SL, SL), SL)]
        return copy_to(src, kvb[h].at[me], cs.at[h, rel], cr.at[h, rel], row_dev(slot))

    def scatter_wait(h, rel):
        ref = kvb[h].at[p * 8 + slot_at(8 - rel)]
        copy_to(ref, ref, cs.at[h, rel], cr.at[h, rel], row_dev(s)).wait_recv()

    for h in range(2):
        for rel in range(1, 8):
            go(scatter(h, rel))
        own_kv[h].start()
    for load in loads:
        load.start()

    def z_rows(h, z):
        return kvb[h].at[pl.ds(pl.multiple_of(z * 8, 8), 8)]

    def z_copy(h, k, which):
        if which == "first":
            ref, target, sem, at = z_rows(h, p), zo[0], 0, 0
        elif which == "second":
            ref, target, sem, at = z_rows(h, p), 3 - p, 1, 1
        else:
            ref, target, sem = z_rows(h, zo[k]), (3 - p if k == 0 else 3 * p - 3), 2 + k
            at = (2, 1, 2)[k]
        return copy_to(ref, ref, zs.at[h, sem], zr.at[h, at], z_dev(target))

    def z_own(h):
        for rel in range(1, 8):
            scatter_wait(h, rel)
        own_kv[h].wait()
        go(z_copy(h, 0, "first"))

        @pl.when(mid)
        def _():
            z_copy(h, 0, "second").start()

    def z_step(h, k):
        ref = z_rows(h, zo[k])
        copy_to(ref, ref, zs.at[h, 0], zr.at[h, k], z_dev(p)).wait_recv()

        @pl.when(mid)
        def _():
            z_copy(h, k, "relay").start()

    def hid_wait(i, holder):
        ref = hbuf.at[holder]
        copy_to(ref, ref, hs.at[i], hr.at[i], tp_dev(t)).wait_recv()

    acc[...] = jnp.zeros_like(acc)
    for i in range(TP * FEAT // HD):
        at = slice(i * HD, (i + 1) * HD)
        spread = jnp.where(eye, jnp.broadcast_to(gain_ref[:, at], (HD, HD)), 0.0)
        gcol[at, :] = jnp.broadcast_to(jnp.sum(spread, axis=1, keepdims=True), (HD, HD))

    def project(holder, row_scale):
        at = pl.ds(pl.multiple_of(holder * FEAT, FEAT), FEAT)
        gain = gcol[at, :]
        normed = hbuf[holder].astype(F32) * row_scale * jnp.concatenate([gain, gain], axis=1)
        acc[...] += lax.dot_general(
            normed.astype(BF), wbuf[at, :], (((0,), (0,)), ((), ())), preferred_element_type=F32
        )

    vscr[...] = jnp.ones_like(vscr)

    for load in loads:
        load.wait()
    for i in range(1, TP):
        sq_wait(i)
    total = sq[0]
    for i in range(1, TP):
        total = total + sq[i]
    row_scale = lax.rsqrt(total[0:1, :] / (TP * FEAT) + 1e-6)
    project(t, row_scale)
    hid_wait(0, partner)
    for i, o in enumerate(ys):
        go(hid_copy(4 + i, hbuf.at[partner], partner, zh * 4 + o))
    z_own(0)
    project(partner, row_scale)
    for i in range(3):
        hid_wait(1 + i, zh * 4 + yin[i])
        project(zh * 4 + yin[i], row_scale)
    z_step(0, 0)
    for i in range(3):
        hid_wait(4 + i, (1 - zh) * 4 + yin[i])
        project((1 - zh) * 4 + yin[i], row_scale)
    z_step(0, 1)
    z_own(1)

    cosine, sine = cos_ref[...], sin_ref[...]
    live = lax.broadcasted_iota(jnp.int32, (ROWS, HD), 0) < length_ref[me]

    def rotated(at):
        x = acc[:, at : at + HD]
        return x * cosine + pltpu.roll(x, 64, 1) * sine

    for h in range(2):
        for g in range(2):
            q = (rotated((2 * h + g) * HD) * (1.0 / 12.0)).astype(BF)
            qb[h][s, g * ROWS : (g + 1) * ROWS, :] = q
    for h in range(2):
        key_ref[:, h * HD : (h + 1) * HD] = jnp.where(live, rotated(512 + h * HD), 0.0).astype(BF)
        v = acc[:, 768 + h * HD : 768 + (h + 1) * HD]
        val_ref[:, h * HD : (h + 1) * HD] = jnp.where(live, v, 0.0).astype(BF)

    def q_copy(h, slot, sem, rel, dev):
        ref = qb[h].at[slot]
        return copy_to(ref, ref, qs.at[h, sem], qr.at[h, rel], dev)

    def q_wait(h, rel):
        ref = qb[h].at[slot_at(rel)]
        copy_to(ref, ref, qs.at[h, 0], qr.at[h, rel], row_dev(s)).wait_recv()

    def sib_rel(rel):
        return (rel + 2 * c + 7) % 8

    for h in range(2):
        for n, rel in enumerate((2, 6, 4)):
            go(q_copy(h, s, n, 8 - rel, row_dev(slot_at(rel))))
        go(q_copy(h, s, 3, sib_rel(0), (sibling, t)))

    def weigh(scores):
        return jnp.exp2(jnp.tanh(scores * (1.0 / 50.0)) * (50.0 * LOG2E))

    contract = (((1,), (1,)), ((), ()))
    row_id = lax.broadcasted_iota(jnp.int32, (2 * ROWS, ROWS), 0) % ROWS
    col_id = lax.broadcasted_iota(jnp.int32, (2 * ROWS, ROWS), 1)
    causal = row_id >= col_id
    ones = jnp.ones((ROWS, HD), BF)
    for h in range(2):
        scores = lax.dot_general(
            qb[h][s], key_ref[:, h * HD : (h + 1) * HD], contract, preferred_element_type=F32
        )
        w = jnp.where(causal, weigh(scores), 0.0).astype(BF)
        values = jnp.concatenate([val_ref[:, h * HD : (h + 1) * HD], ones], axis=1)
        both = jnp.dot(w, values, preferred_element_type=F32)
        snum[h] = both[:, :HD]
        sden[h] = both[:, HD:]
    z_step(0, 2)

    for h in range(2):
        for n, rel in enumerate((2, 6, 4)):
            q_wait(h, rel)
            go(q_copy(h, slot_at(rel), 4 + n, sib_rel(rel), (sibling, t)))

    def q_waits(h):
        for rel in (1, 3, 5, 7):
            q_wait(h, rel)

    def attend(h, slot, num_at, den_at):
        group = group_ref[p * 8 + slot]
        for j in range(8):
            block = kvb[h][owner_ref[group, j]]
            kscr[j * SL : (j + 1) * SL, :] = block[:, :HD]
            vscr[j * SL : (j + 1) * SL, :HD] = block[:, HD:]
        scores = lax.dot_general(qb[h][slot], kscr[...], contract, preferred_element_type=F32)
        both = jnp.dot(weigh(scores).astype(BF), vscr[...], preferred_element_type=F32)
        num_at[...] = both[:, :HD].astype(BF)
        for g in range(4):
            den = both[g * HD : (g + 1) * HD, HD:]
            den_at[g : g + 1, :] = jnp.sum(jnp.where(eye, den, 0.0), axis=0, keepdims=True)

    def back_num(h, rel):
        slot = slot_at(rel)
        return copy_to(ns[h].at[slot], nr[h].at[s], rs.at[h, rel], rr.at[h, rel], row_dev(slot))

    def back_den(h, rel):
        slot = slot_at(rel)
        return copy_to(ds[h].at[slot], dr[h].at[s], es.at[h, rel], er.at[h, rel], row_dev(slot))

    def attend_loop(h, first, last):
        @pl.loop(first, last)
        def _(rel):
            slot = slot_at(rel)
            attend(h, slot, ns[h].at[slot], ds[h].at[slot])
            back_num(h, rel).start()
            back_den(h, rel).start()

    def combine(h):
        for rel in range(1, 8):
            src = slot_at(8 - rel)
            copy_to(nr[h].at[src], nr[h].at[src], rs.at[h, rel], rr.at[h, rel], row_dev(s)).wait_recv()
            copy_to(dr[h].at[src], dr[h].at[src], es.at[h, rel], er.at[h, rel], row_dev(s)).wait_recv()
        den_rows = dr[h][0]
        for i in range(1, 8):
            den_rows = den_rows + dr[h][i]
        for g in range(4):
            at = slice(g * HD, (g + 1) * HD)
            spread = jnp.where(eye, jnp.broadcast_to(den_rows[g : g + 1, :], (HD, HD)), 0.0)
            den = jnp.sum(spread, axis=1, keepdims=True) + sden[h, at, :]
            num = snum[h, at, :]
            for i in range(8):
                num = num + nr[h][i, at, :].astype(F32)
            r0 = (g % 2) * HD
            head = 2 * h + g // 2
            rows_live = (lax.broadcasted_iota(jnp.int32, (HD, HD), 0) + r0) < length_ref[me]
            out = jnp.where(rows_live, num / den, 0.0).astype(BF)
            att_ref[r0 : r0 + HD, head * HD : (head + 1) * HD] = out

    q_waits(0)
    attend_loop(0, 1, 3)
    z_step(1, 0)
    attend_loop(0, 3, 6)
    z_step(1, 1)
    attend_loop(0, 6, 8)
    attend(0, s, nr[0].at[s], dr[0].at[s])
    q_waits(1)
    z_step(1, 2)
    attend_loop(1, 1, 8)
    attend(1, s, nr[1].at[s], dr[1].at[s])
    combine(0)
    combine(1)

    for copy in pending:
        copy.wait_send()
    for h in range(2):
        for rel in range(1, 8):
            back_num(h, rel).wait_send()
            back_den(h, rel).wait_send()

    @pl.when(mid)
    def _():
        for h in range(2):
            z_copy(h, 0, "second").wait_send()
            for k in range(3):
                z_copy(h, k, "relay").wait_send()


def body(hidden, norm_gain, w_query, w_key, w_value, prefix_kv, group_of, block_owner, lengths):
    kv = prefix_kv.reshape(512, 2, 2, HD).transpose(2, 0, 1, 3).reshape(2, 512, 2 * HD)
    gain = norm_gain.reshape(1, TP * FEAT)
    full_cos, signed_sin = rope_constants()
    smem = pl.BlockSpec(memory_space=pltpu.SMEM)
    vmem = pl.BlockSpec(memory_space=pltpu.VMEM)
    hbm = pl.BlockSpec(memory_space=pl.ANY)
    dma = pltpu.SemaphoreType.DMA
    pair = lambda shape, dtype: [pltpu.VMEM(shape, dtype)] * 2
    return pl.pallas_call(
        kernel,
        out_shape=(
            jax.ShapeDtypeStruct((ROWS, 512), BF),
            jax.ShapeDtypeStruct((ROWS, 256), BF),
            jax.ShapeDtypeStruct((ROWS, 256), BF),
        ),
        in_specs=[smem] * 3 + [hbm] * 5 + [vmem] * 3,
        out_specs=(vmem, vmem, vmem),
        scratch_shapes=[
            pltpu.VMEM((TP, FEAT, ROWS), BF),
            pltpu.VMEM((TP * FEAT, 1024), BF),
            *pair((32, SL, 256), BF),
            *pair((8, 512, HD), BF),
            *pair((8, 512, HD), BF),
            *pair((8, 512, HD), BF),
            *pair((8, 8, HD), F32),
            *pair((8, 8, HD), F32),
            pltpu.VMEM((ROWS, 1024), F32),
            pltpu.VMEM((TP, 8, ROWS), F32),
            pltpu.VMEM((TP * FEAT, HD), F32),
            pltpu.VMEM((512, HD), BF),
            pltpu.VMEM((512, 2 * HD), BF),
            pltpu.VMEM((2, 512, HD), F32),
            pltpu.VMEM((2, 512, HD), F32),
            dma((3,)), dma((3,)), dma((8,)), dma((8,)), dma((7,)), dma((7,)),
            dma((2, 8)), dma((2, 8)), dma((2, 5)), dma((2, 3)),
            dma((2, 8)), dma((2, 8)), dma((2, 8)), dma((2, 8)), dma((2, 8)), dma((2, 8)),
        ],
        name="prefill",
        compiler_params=pltpu.CompilerParams(
            collective_id=1, has_side_effects=True, vmem_limit_bytes=56 * 2**20
        ),
    )(
        group_of, block_owner, lengths, hidden.T, w_query, w_key, w_value, kv, gain,
        jnp.asarray(full_cos), jnp.asarray(signed_sin),
    )


def solution(mesh):
    in_specs = (
        P("req", "tp"), P(), P(None, "tp"), P(None, "tp"), P(None, "tp"),
        P("req", None, "tp"), P(), P(), P(),
    )
    out_specs = (P("req", "tp"), P("req", "tp"), P("req", "tp"))
    return jax.shard_map(body, mesh=mesh, in_specs=in_specs, out_specs=out_specs, check_vma=False)
```

time: 568 us -> 103 us (0.18)
  waiting for transfers between devices: 392 us -> 0 us
  local copies, waits for them, and re-layouts: 104 us -> 7.69 us
  Pallas kernels: 0 us -> 94 us
  matrix products: 38.6 us -> 0 us
  between operations: 14 us -> 0.65 us
  other arithmetic: 12.9 us -> 0 us
    reduce_scatter x1 -> x0, waiting for transfers between devices: 170 us -> none  [body(): lax.psum_scatter(full_num.reshape(device_count * row_count, -1), 'req', s...]
    all_gather x2 -> x0, waiting for transfers between devices: 160 us -> none  [the longest x1 83.8 us: body(): gathered = lax.all_gather(hidden, 'tp', axis=1, tiled=True)]
    pallas_call x0 -> x1, Pallas kernels: none -> 94 us  [body(): pl.pallas_call(kernel, out_shape=(jax.ShapeDtypeStruct((ROWS, 512), BF),...]
    unnamed x5 -> x0, waiting for transfers between devices: 62.1 us -> none
    reshape x7 -> x2, local copies, waits for them, and re-layouts: 47.3 us -> 2.52 us  [the longest x1 1.4 us: body(): gain = norm_gain.reshape(1, TP * FEAT)]
    dot_general x7 -> x0, matrix products: 38.6 us -> none  [the longest x2 14.4 us: attend(): jnp.einsum('kgrc,ckd->rkgd', weights.astype(jnp.bfloat16), value_block, p...]
    unnamed x30 -> x5, local copies, waits for them, and re-layouts: 27.2 us -> 4.81 us
    scatter x2 -> x0, local copies, waits for them, and re-layouts: 8.8 us -> none  [the longest x1 8.07 us: body(): full_num.at[members]]
  transfers between devices with their start and end apart: 4 -> 0, of which waited for: 4 -> 0; matrix products, arithmetic and copies ran while one was open for 17% -> 0% of each run, Pallas kernels for 0% -> 0%
where the time goes in v1:
time: 103 us; the launch traced here: 102 us
  Pallas kernels  94 us (91%)
  local copies, waits for them, and re-layouts  7.69 us (7%)
    pallas_call x1, Pallas kernels, body(): pl.pallas_call(kernel, out_shape=(jax.ShapeDtypeStruct((ROWS, 512), BF),...  94 us
    unnamed x5, local copies, waits for them, and re-layouts  4.81 us

profile of v1, /device:TPU:1, one launch (start us, length us, event | category | flops | bytes accessed | tf_op | source)
XLA Modules:
  0.0 102.3 jit_solution(14227007232628881724)
XLA Ops:
  0.6 0.0 copy-start
  0.6 1.4 %reshape.17.gain_ref = f32[1,4608]{1,0:T(1,128)} reshape(f32[4608]{0:T(1024)} %param.12) | data formatting | bytes 36864 | tf_op jit(solution)/shard_map/reshape | solution.py:353
  2.0 0.0 copy-done
  2.1 0.4 bitcast_bitcast_fusion
  2.4 1.1 %reshape.16.kv = bf16[2,512,256]{2,1,0:T(8,128)(2,1)} reshape(bf16[2,512,2,128]{3,2,1,0:T(2,128)(2,1)S(1)} %bitcast_bitcast_fusion) | data formatting | bytes 1048576 | tf_op jit(solution)/shard_map/reshape | solution.py:352
  3.5 94.0 %prefill.1 = (bf16[256,512]{1,0:T(8,128)(2,1)}, bf16[256,256]{1,0:T(8,128)(2,1)}, bf16[256,256]{1,0:T(8,128)(2,1)}) custom-call(s32[32]{0:T(128)} %group_ref.1, s32[4,8]{1,0:T(4,128)} %owner_ref.1, s32[32]{0:T(128)} %length_ref.1, bf16[576,256]{1,0:T(8,128)(2,1)} %bitcast.8, bf16[4608,512]{1,0:T(8,128)(2,1)} %wq.1, bf16[4608,256]{1,0:T(8,128)(2,1)} %wk.1, ...), custom_call_target="tpu_custom_call" | custom-call | tf_op jit(solution)/shard_map/prefill/pallas_call | solution.py:360
  97.5 1.7 %copy.20 = bf16[256,512]{1,0:T(8,128)(2,1)} copy(bf16[256,512]{1,0:T(8,128)(2,1)} %get-tuple-element.6) | data formatting | bytes 524288
  99.2 1.6 %copy.21 = bf16[256,256]{1,0:T(8,128)(2,1)} copy(bf16[256,256]{1,0:T(8,128)(2,1)} %get-tuple-element.7) | data formatting | bytes 262144
  100.7 1.6 %copy.22 = bf16[256,256]{1,0:T(8,128)(2,1)} copy(bf16[256,256]{1,0:T(8,128)(2,1)} %get-tuple-element.8) | data formatting | bytes 262144
Async XLA Ops:
  0.6 1.4 %copy-start = (bf16[512,2,256]{2,1,0:T(2,128)(2,1)S(1)}, bf16[512,2,256]{2,1,0:T(2,128)(2,1)}, u32[]{:S(2)}) copy-start(bf16[512,2,256]{2,1,0:T(2,128)(2,1)} %param.16) | copy-start | bytes 1572868

commit v2 on v1

v2 whole, which is shorter than its diff:
```python
import functools
import math

import jax
import jax.numpy as jnp
import numpy as np
from jax import lax
from jax.experimental import pallas as pl
from jax.experimental.pallas import tpu as pltpu
from jax.sharding import PartitionSpec as P

MESH = pl.DeviceIdType.MESH
BF = jnp.bfloat16
F32 = jnp.float32
HD = 128
ROWS = 256
PREFIX = 4096
FEAT = 576
TP = 8
SL = 64
LOG2E = 1.4426950408889634


def rope_constants():
    freq = np.exp(np.arange(64, dtype=np.float32) * np.float32(-2.0 * math.log(10000.0) / 128))
    angle = (np.arange(ROWS) + PREFIX).astype(np.float32)[:, None] * freq[None, :]
    cosine, sine = np.cos(angle.astype(np.float64)), np.sin(angle.astype(np.float64))
    full_cos = np.concatenate([cosine, cosine], axis=1).astype(np.float32)
    signed_sin = np.concatenate([-sine, sine], axis=1).astype(np.float32)
    return full_cos, signed_sin


def kernel(
    group_ref, owner_ref, length_ref, hid, wq, wk, wv, kv, gain_ref, cos_ref, sin_ref,
    att_ref, key_ref, val_ref,
    hbuf, wbuf, kraw, kf32, kvs, kvb0, kvb1, qb0, qb1, ns0, ns1, nl0, nl1, ds0, ds1, dl0, dl1,
    acc, sq, gcol, kscr, vscr, snum, sden,
    lsem, wsem, qss, qsr, hs, hr, cs, cr, zs, zr, qs, qr, rs, rr, es, er,
):
    kvb, qb, ns, nl, ds, dl = (kvb0, kvb1), (qb0, qb1), (ns0, ns1), (nl0, nl1), (ds0, ds1), (dl0, dl1)
    me = lax.axis_index("req")
    t = lax.axis_index("tp")
    p, s = me // 8, me % 8
    x, c = s // 2, s % 2
    zh, y = t // 4, t % 4
    inner = (p * (3 - p)) // 2
    mid = inner == 1
    zo = (p + 1 - 2 * (p % 2), 2 - p // 2, 3 - 3 * (p // 2))

    def row_dev(slot):
        return (p * 8 + slot, t)

    def z_dev(z):
        return (z * 8 + s, t)

    def tp_dev(other):
        return (me, other)

    def slot_at(rel):
        return (s + rel) % 8

    def copy_to(src, dst, send, recv, dev):
        return pltpu.make_async_remote_copy(src, dst, send, recv, device_id=dev, device_id_type=MESH)

    sibling = p * 8 + s + 1 - 2 * c
    here, there = zh * 4, (1 - zh) * 4
    yp, ym, yq = (y + 1) % 4, (y + 3) % 4, (y + 2) % 4

    own_hid = pltpu.make_async_copy(hid, hbuf.at[t], lsem.at[0])
    own_hid.start()
    own_kv = pltpu.make_async_copy(kv, kraw, lsem.at[1])
    own_kv.start()
    loads = [
        pltpu.make_async_copy(wq, wbuf.at[:, 0:512], wsem.at[0]),
        pltpu.make_async_copy(wk, wbuf.at[:, 512:768], wsem.at[1]),
        pltpu.make_async_copy(wv, wbuf.at[:, 768:1024], wsem.at[2]),
    ]
    for load in loads:
        load.start()

    barrier = pltpu.get_barrier_semaphore()
    greet = [row_dev(slot_at(rel)) for rel in range(1, 8)]
    greet += [z_dev(zo[0])] + [tp_dev((t + i) % TP) for i in range(1, TP)]
    for dev in greet:
        pl.semaphore_signal(barrier, inc=1, device_id=dev, device_id_type=MESH)

    @pl.when(mid)
    def _():
        pl.semaphore_signal(barrier, inc=1, device_id=z_dev(3 - p), device_id_type=MESH)

    eye = lax.broadcasted_iota(jnp.int32, (HD, HD), 0) == lax.broadcasted_iota(jnp.int32, (HD, HD), 1)
    own_hid.wait()
    features = hbuf[t].astype(F32)
    sq[t] = jnp.broadcast_to(jnp.sum(features * features, axis=0, keepdims=True), (8, ROWS))
    own_kv.wait()
    for h in range(2):
        kf32[...] = kraw[:, :, h * HD : (h + 1) * HD].astype(F32).reshape(1024, HD)
        kvs[h, :, :HD] = kf32[pl.ds(0, 512, stride=2), :].astype(BF)
        kvs[h, :, HD:] = kf32[pl.ds(1, 512, stride=2), :].astype(BF)
    for h in range(2):
        kvb[h][me] = kvs[h, pl.ds(pl.multiple_of(s * SL, SL), SL), :]
    pl.semaphore_wait(barrier, len(greet) + inner)

    pending = []

    def go(copy):
        copy.start()
        pending.append(copy)

    def hid_ref(holder, half):
        if half is None:
            return hbuf.at[holder]
        return hbuf.at[holder, pl.ds(half * (FEAT // 2), FEAT // 2)]

    def hid_copy(i, holder, half, dev):
        ref = hid_ref(holder, half)
        go(copy_to(ref, ref, hs.at[i], hr.at[i], tp_dev(dev)))

    def hid_wait(i, holder, half):
        ref = hid_ref(holder, half)
        copy_to(ref, ref, hs.at[i], hr.at[i], tp_dev(t)).wait_recv()

    def sq_copy(i):
        return copy_to(sq.at[t], sq.at[t], qss.at[i], qsr.at[i], tp_dev((t + i) % TP))

    def sq_wait(i):
        ref = sq.at[(t + TP - i) % TP]
        copy_to(ref, ref, qss.at[i], qsr.at[i], tp_dev(t)).wait_recv()

    def scatter(h, rel):
        slot = slot_at(rel)
        src = kvs.at[h, pl.ds(pl.multiple_of(slot * SL, SL), SL)]
        return copy_to(src, kvb[h].at[me], cs.at[h, rel], cr.at[h, rel], row_dev(slot))

    def scatter_wait(h, rel):
        ref = kvb[h].at[p * 8 + slot_at(8 - rel)]
        copy_to(ref, ref, cs.at[h, rel], cr.at[h, rel], row_dev(s)).wait_recv()

    def z_rows(h, z):
        return kvb[h].at[pl.ds(pl.multiple_of(z * 8, 8), 8)]

    def z_copy(h, k, which):
        if which == "first":
            ref, target, sem, at = z_rows(h, p), zo[0], 0, 0
        elif which == "second":
            ref, target, sem, at = z_rows(h, p), 3 - p, 1, 1
        else:
            ref, target, sem = z_rows(h, zo[k]), (3 - p if k == 0 else 3 * p - 3), 2 + k
            at = (2, 1, 2)[k]
        return copy_to(ref, ref, zs.at[h, sem], zr.at[h, at], z_dev(target))

    def z_own(h):
        go(z_copy(h, 0, "first"))

        @pl.when(mid)
        def _():
            z_copy(h, 0, "second").start()

    def z_step(h, k):
        ref = z_rows(h, zo[k])
        copy_to(ref, ref, zs.at[h, 0], zr.at[h, k], z_dev(p)).wait_recv()

        @pl.when(mid)
        def _():
            z_copy(h, k, "relay").start()

    def project(holder, row_scale):
        at = pl.ds(pl.multiple_of(holder * FEAT, FEAT), FEAT)
        gain = gcol[at, :]
        normed = hbuf[holder].astype(F32) * row_scale * jnp.concatenate([gain, gain], axis=1)
        acc[...] += lax.dot_general(
            normed.astype(BF), wbuf[at, :], (((0,), (0,)), ((), ())), preferred_element_type=F32
        )

    for i in range(1, TP):
        go(sq_copy(i))
    hid_copy(0, t, 0, there + y)
    hid_copy(1, t, 1, there + y)
    hid_copy(2, t, None, here + yp)
    hid_copy(3, t, None, here + ym)
    for h in range(2):
        for rel in range(1, 8):
            go(scatter(h, rel))

    acc[...] = jnp.zeros_like(acc)
    vscr[...] = jnp.ones_like(vscr)
    for i in range(TP * FEAT // HD):
        at = slice(i * HD, (i + 1) * HD)
        spread = jnp.where(eye, jnp.broadcast_to(gain_ref[:, at], (HD, HD)), 0.0)
        gcol[at, :] = jnp.broadcast_to(jnp.sum(spread, axis=1, keepdims=True), (HD, HD))

    hid_wait(2, here + ym, None)
    hid_copy(4, here + ym, 0, here + yp)
    hid_wait(3, here + yp, None)
    hid_copy(5, here + yp, 1, here + ym)
    for h in range(2):
        for rel in range(1, 8):
            scatter_wait(h, rel)
    hid_wait(0, there + y, 0)
    hid_copy(6, there + y, 0, here + yp)
    hid_copy(7, there + y, 0, here + ym)
    z_own(0)
    for i in range(1, TP):
        sq_wait(i)
    total = sq[0]
    for i in range(1, TP):
        total = total + sq[i]
    row_scale = lax.rsqrt(total[0:1, :] / (TP * FEAT) + 1e-6)
    for load in loads:
        load.wait()
    project(t, row_scale)
    hid_wait(1, there + y, 1)
    hid_copy(8, there + y, 1, here + yp)
    hid_copy(9, there + y, 1, here + ym)
    hid_wait(6, there + ym, 0)
    hid_copy(10, there + ym, 0, here + yp)
    project(here + ym, row_scale)
    project(here + yp, row_scale)
    hid_wait(9, there + yp, 1)
    hid_copy(11, there + yp, 1, here + ym)
    z_step(0, 0)
    project(there + y, row_scale)
    hid_wait(4, here + yq, 0)
    hid_wait(5, here + yq, 1)
    project(here + yq, row_scale)
    hid_wait(8, there + ym, 1)
    project(there + ym, row_scale)
    hid_wait(7, there + yp, 0)
    project(there + yp, row_scale)
    hid_wait(10, there + yq, 0)
    hid_wait(11, there + yq, 1)
    z_step(0, 1)
    z_own(1)
    project(there + yq, row_scale)

    cosine, sine = cos_ref[...], sin_ref[...]
    live = lax.broadcasted_iota(jnp.int32, (ROWS, HD), 0) < length_ref[me]

    def rotated(at):
        v = acc[:, at : at + HD]
        return v * cosine + pltpu.roll(v, 64, 1) * sine

    def q_copy(h, slot, sem, rel, dev):
        ref = qb[h].at[slot]
        return copy_to(ref, ref, qs.at[h, sem], qr.at[h, rel], dev)

    def q_wait(h, rel):
        ref = qb[h].at[slot_at(rel)]
        copy_to(ref, ref, qs.at[h, 0], qr.at[h, rel], row_dev(s)).wait_recv()

    def sib_rel(rel):
        return (rel + 2 * c + 7) % 8

    def weigh(scores):
        return jnp.exp2(jnp.tanh(scores * (1.0 / 50.0)) * (50.0 * LOG2E))

    contract = (((1,), (1,)), ((), ()))
    for h in range(2):
        for g in range(2):
            q = (rotated((2 * h + g) * HD) * (1.0 / 12.0)).astype(BF)
            qb[h][s, g * ROWS : (g + 1) * ROWS, :] = q
    for h in range(2):
        key_ref[:, h * HD : (h + 1) * HD] = jnp.where(live, rotated(512 + h * HD), 0.0).astype(BF)
        v = acc[:, 768 + h * HD : 768 + (h + 1) * HD]
        val_ref[:, h * HD : (h + 1) * HD] = jnp.where(live, v, 0.0).astype(BF)
        for n, rel in enumerate((2, 6, 4)):
            go(q_copy(h, s, n, 8 - rel, row_dev(slot_at(rel))))
        go(q_copy(h, s, 3, sib_rel(0), (sibling, t)))
    z_step(0, 2)

    row_id = lax.broadcasted_iota(jnp.int32, (2 * ROWS, ROWS), 0) % ROWS
    col_id = lax.broadcasted_iota(jnp.int32, (2 * ROWS, ROWS), 1)
    causal = row_id >= col_id
    ones = jnp.ones((ROWS, HD), BF)
    for h in range(2):
        scores = lax.dot_general(
            qb[h][s], key_ref[:, h * HD : (h + 1) * HD], contract, preferred_element_type=F32
        )
        w = jnp.where(causal, weigh(scores), 0.0).astype(BF)
        values = jnp.concatenate([val_ref[:, h * HD : (h + 1) * HD], ones], axis=1)
        both = jnp.dot(w, values, preferred_element_type=F32)
        snum[h] = both[:, :HD]
        sden[h] = both[:, HD:]

    def q_forward(h):
        for n, rel in enumerate((2, 6, 4)):
            q_wait(h, rel)
            go(q_copy(h, slot_at(rel), 4 + n, sib_rel(rel), (sibling, t)))

    def q_rest(h):
        for rel in (1, 3, 5, 7):
            q_wait(h, rel)

    def num_copy(h, i, dev):
        return copy_to(ns[h].at[i], nl[h].at[i], rs.at[h, i], rr.at[h, i], dev)

    def den_copy(h, i, dev):
        return copy_to(ds[h].at[i], dl[h].at[i], es.at[h, i], er.at[h, i], dev)

    def land_wait(h, i):
        num_copy(h, i, row_dev(s)).wait_recv()
        den_copy(h, i, row_dev(s)).wait_recv()

    def attend_loop(h, first, last):
        @pl.loop(first, last)
        def _(i):
            dx = (i + 1) % 4
            core = (1 - c) + (i // 4) * (2 * c - 1)
            slot = ((x + dx) % 4) * 2 + core
            group = group_ref[p * 8 + slot]
            for j in range(8):
                block = kvb[h][owner_ref[group, j]]
                kscr[j * SL : (j + 1) * SL, :] = block[:, :HD]
                vscr[j * SL : (j + 1) * SL, :HD] = block[:, HD:]
            scores = lax.dot_general(qb[h][slot], kscr[...], contract, preferred_element_type=F32)
            both = jnp.dot(weigh(scores).astype(BF), vscr[...], preferred_element_type=F32)

            @pl.when(i < 7)
            def _():
                num = both[:, :HD]
                for g in range(4):
                    den = both[g * HD : (g + 1) * HD, HD:]
                    ds[h][i, g : g + 1, :] = jnp.sum(jnp.where(eye, den, 0.0), axis=0, keepdims=True)

                @pl.when(i < 4)
                def _():
                    ns[h][i] = num.astype(BF)
                    num_copy(h, i, (sibling, t)).start()
                    den_copy(h, i, (sibling, t)).start()

                @pl.when(i >= 4)
                def _():
                    land_wait(h, i - 4)
                    ns[h][i] = (num + nl[h][i - 4].astype(F32)).astype(BF)
                    ds[h][i] = ds[h][i] + dl[h][i - 4]
                    num_copy(h, i, row_dev(slot)).start()
                    den_copy(h, i, row_dev(slot)).start()

            @pl.when(i == 7)
            def _():
                snum[h] += both[:, :HD]
                sden[h] += both[:, HD:]

    def combine(h):
        for i in range(3, 7):
            land_wait(h, i)
        den_rows = dl[h][3] + dl[h][4] + dl[h][5] + dl[h][6]
        for g in range(4):
            at = slice(g * HD, (g + 1) * HD)
            spread = jnp.where(eye, jnp.broadcast_to(den_rows[g : g + 1, :], (HD, HD)), 0.0)
            den = jnp.sum(spread, axis=1, keepdims=True) + sden[h, at, :]
            num = snum[h, at, :]
            for i in range(3, 7):
                num = num + nl[h][i, at, :].astype(F32)
            r0 = (g % 2) * HD
            head = 2 * h + g // 2
            rows_live = (lax.broadcasted_iota(jnp.int32, (HD, HD), 0) + r0) < length_ref[me]
            out = jnp.where(rows_live, num / den, 0.0).astype(BF)
            att_ref[r0 : r0 + HD, head * HD : (head + 1) * HD] = out

    q_forward(0)
    q_rest(0)
    attend_loop(0, 0, 3)
    q_forward(1)
    z_step(1, 0)
    attend_loop(0, 3, 8)
    z_step(1, 1)
    q_rest(1)
    combine(0)
    z_step(1, 2)
    attend_loop(1, 0, 8)
    combine(1)

    for copy in pending:
        copy.wait_send()
    for h in range(2):
        for i in range(7):
            num_copy(h, i, row_dev(s)).wait_send()
            den_copy(h, i, row_dev(s)).wait_send()

    @pl.when(mid)
    def _():
        for h in range(2):
            z_copy(h, 0, "second").wait_send()
            for k in range(3):
                z_copy(h, k, "relay").wait_send()


def finish(att, key, val, att_out, key_out, val_out):
    att_out[...] = att[...]
    key_out[...] = key[...]
    val_out[...] = val[...]


def body(hidden, norm_gain, w_query, w_key, w_value, prefix_kv, group_of, block_owner, lengths):
    gain = norm_gain.reshape(1, TP * FEAT)
    full_cos, signed_sin = rope_constants()
    smem = pl.BlockSpec(memory_space=pltpu.SMEM)
    vmem = pl.BlockSpec(memory_space=pltpu.VMEM)
    hbm = pl.BlockSpec(memory_space=pl.ANY)
    dma = pltpu.SemaphoreType.DMA
    pair = lambda shape, dtype: [pltpu.VMEM(shape, dtype)] * 2
    shapes = tuple(jax.ShapeDtypeStruct((ROWS, n), BF) for n in (512, 256, 256))
    results = pl.pallas_call(
        kernel,
        out_shape=shapes,
        in_specs=[smem] * 3 + [hbm] * 5 + [vmem] * 3,
        out_specs=(vmem, vmem, vmem),
        scratch_shapes=[
            pltpu.VMEM((TP, FEAT, ROWS), BF),
            pltpu.VMEM((TP * FEAT, 1024), BF),
            pltpu.VMEM((512, 2, 256), BF),
            pltpu.VMEM((1024, HD), F32),
            pltpu.VMEM((2, 512, 256), BF),
            *pair((32, SL, 256), BF),
            *pair((8, 512, HD), BF),
            *pair((8, 512, HD), BF),
            *pair((8, 512, HD), BF),
            *pair((8, 8, HD), F32),
            *pair((8, 8, HD), F32),
            pltpu.VMEM((ROWS, 1024), F32),
            pltpu.VMEM((TP, 8, ROWS), F32),
            pltpu.VMEM((TP * FEAT, HD), F32),
            pltpu.VMEM((512, HD), BF),
            pltpu.VMEM((512, 2 * HD), BF),
            pltpu.VMEM((2, 512, HD), F32),
            pltpu.VMEM((2, 512, HD), F32),
            dma((2,)), dma((3,)), dma((8,)), dma((8,)), dma((12,)), dma((12,)),
            dma((2, 8)), dma((2, 8)), dma((2, 5)), dma((2, 3)),
            dma((2, 8)), dma((2, 8)), dma((2, 8)), dma((2, 8)), dma((2, 8)), dma((2, 8)),
        ],
        name="prefill",
        compiler_params=pltpu.CompilerParams(
            collective_id=1, has_side_effects=True, vmem_limit_bytes=56 * 2**20
        ),
    )(
        group_of, block_owner, lengths, hidden.T, w_query, w_key, w_value, prefix_kv, gain,
        jnp.asarray(full_cos), jnp.asarray(signed_sin),
    )
    return pl.pallas_call(
        finish, out_shape=shapes, in_specs=[vmem] * 3, out_specs=(vmem, vmem, vmem), name="finish"
    )(*results)


def solution(mesh):
    in_specs = (
        P("req", "tp"), P(), P(None, "tp"), P(None, "tp"), P(None, "tp"),
        P("req", None, "tp"), P(), P(), P(),
    )
    out_specs = (P("req", "tp"), P("req", "tp"), P("req", "tp"))
    return jax.shard_map(body, mesh=mesh, in_specs=in_specs, out_specs=out_specs, check_vma=False)
```

time: 103 us -> 86.5 us (0.84)
  Pallas kernels: 94 us -> 84.4 us
  local copies, waits for them, and re-layouts: 7.69 us -> 1.35 us
    pallas_call x1 -> x2, Pallas kernels: 94 us -> 84.4 us  [the longest x1 82.5 us: body(): pl.pallas_call(kernel, out_shape=shapes, in_specs=[smem] * 3 + [hbm] * 5...]
    unnamed x5 -> x0, local copies, waits for them, and re-layouts: 4.81 us -> none
    reshape x1 -> x0, local copies, waits for them, and re-layouts: 1.11 us -> none  [body(): prefix_kv.reshape(512, 2, 2, HD).transpose(2, 0, 1, 3)]
where the time goes in v2:
time: 86.5 us; the launch traced here: 86.4 us
  Pallas kernels  84.4 us (98%)
  local copies, waits for them, and re-layouts  1.35 us (2%)
    pallas_call x1, Pallas kernels, body(): pl.pallas_call(kernel, out_shape=shapes, in_specs=[smem] * 3 + [hbm] * 5...  82.5 us
    pallas_call x1, Pallas kernels, body(): pl.pallas_call(finish, out_shape=shapes, in_specs=[vmem] * 3, out_specs=(...  1.84 us

profile of v2, /device:TPU:1, one launch (start us, length us, event | category | flops | bytes accessed | tf_op | source)
XLA Modules:
  0.0 86.4 jit_solution(5380410198823044689)
XLA Ops:
  0.6 1.3 %reshape.9.gain_ref = f32[1,4608]{1,0:T(1,128)} reshape(f32[4608]{0:T(1024)} %param.12) | data formatting | bytes 36864 | tf_op jit(solution)/shard_map/reshape | solution.py:396
  2.0 82.5 %prefill.1 = (bf16[256,512]{1,0:T(8,128)(2,1)}, bf16[256,256]{1,0:T(8,128)(2,1)}, bf16[256,256]{1,0:T(8,128)(2,1)}) custom-call(s32[32]{0:T(128)} %group_ref.1, s32[4,8]{1,0:T(4,128)} %owner_ref.1, s32[32]{0:T(128)} %length_ref.1, bf16[576,256]{1,0:T(8,128)(2,1)} %bitcast.1, bf16[4608,512]{1,0:T(8,128)(2,1)} %wq.1, bf16[4608,256]{1,0:T(8,128)(2,1)} %wk.1, ...), custom_call_target="tpu_custom_call" | custom-call | tf_op jit(solution)/shard_map/prefill/pallas_call | solution.py:404
  84.5 1.8 %finish.1 = (bf16[256,512]{1,0:T(8,128)(2,1)}, bf16[256,256]{1,0:T(8,128)(2,1)}, bf16[256,256]{1,0:T(8,128)(2,1)}) custom-call(bf16[256,512]{1,0:T(8,128)(2,1)} %get-tuple-element.6.att, bf16[256,256]{1,0:T(8,128)(2,1)} %get-tuple-element.7.key, bf16[256,256]{1,0:T(8,128)(2,1)} %get-tuple-element.8.val), custom_call_target="tpu_custom_call" | custom-call | tf_op jit(solution)/shard_map/finish/pallas_call | solution.py:440

commit v3 on v2

--- a/solution.py
+++ b/solution.py
@@ -89,16 +89,6 @@
         pl.semaphore_signal(barrier, inc=1, device_id=z_dev(3 - p), device_id_type=MESH)
 
     eye = lax.broadcasted_iota(jnp.int32, (HD, HD), 0) == lax.broadcasted_iota(jnp.int32, (HD, HD), 1)
-    own_hid.wait()
-    features = hbuf[t].astype(F32)
-    sq[t] = jnp.broadcast_to(jnp.sum(features * features, axis=0, keepdims=True), (8, ROWS))
-    own_kv.wait()
-    for h in range(2):
-        kf32[...] = kraw[:, :, h * HD : (h + 1) * HD].astype(F32).reshape(1024, HD)
-        kvs[h, :, :HD] = kf32[pl.ds(0, 512, stride=2), :].astype(BF)
-        kvs[h, :, HD:] = kf32[pl.ds(1, 512, stride=2), :].astype(BF)
-    for h in range(2):
-        kvb[h][me] = kvs[h, pl.ds(pl.multiple_of(s * SL, SL), SL), :]
     pl.semaphore_wait(barrier, len(greet) + inner)
 
     pending = []
@@ -156,13 +146,22 @@
         def _():
             z_copy(h, 0, "second").start()
 
-    def z_step(h, k):
+    def z_wait(h, k):
         ref = z_rows(h, zo[k])
         copy_to(ref, ref, zs.at[h, 0], zr.at[h, k], z_dev(p)).wait_recv()
 
+    def z_relay(h, *ks):
         @pl.when(mid)
         def _():
-            z_copy(h, k, "relay").start()
+            for k in ks:
+                z_wait(h, k)
+                z_copy(h, k, "relay").start()
+
+    def z_take(h):
+        @pl.when(inner == 0)
+        def _():
+            for k in range(3):
+                z_wait(h, k)
 
     def project(holder, row_scale):
         at = pl.ds(pl.multiple_of(holder * FEAT, FEAT), FEAT)
@@ -172,12 +171,23 @@
             normed.astype(BF), wbuf[at, :], (((0,), (0,)), ((), ())), preferred_element_type=F32
         )
 
+    for half in range(2):
+        src = hid.at[pl.ds(half * (FEAT // 2), FEAT // 2)]
+        go(copy_to(src, hid_ref(t, half), hs.at[half], hr.at[half], tp_dev(there + y)))
+    go(copy_to(hid, hid_ref(t, None), hs.at[2], hr.at[2], tp_dev(here + yp)))
+    go(copy_to(hid, hid_ref(t, None), hs.at[3], hr.at[3], tp_dev(here + ym)))
+    own_hid.wait()
+    features = hbuf[t].astype(F32)
+    sq[t] = jnp.broadcast_to(jnp.sum(features * features, axis=0, keepdims=True), (8, ROWS))
+    own_kv.wait()
+    for h in range(2):
+        kf32[...] = kraw[:, :, h * HD : (h + 1) * HD].astype(F32).reshape(1024, HD)
+        kvs[h, :, :HD] = kf32[pl.ds(0, 512, stride=2), :].astype(BF)
+        kvs[h, :, HD:] = kf32[pl.ds(1, 512, stride=2), :].astype(BF)
+    for h in range(2):
+        kvb[h][me] = kvs[h, pl.ds(pl.multiple_of(s * SL, SL), SL), :]
     for i in range(1, TP):
         go(sq_copy(i))
-    hid_copy(0, t, 0, there + y)
-    hid_copy(1, t, 1, there + y)
-    hid_copy(2, t, None, here + yp)
-    hid_copy(3, t, None, here + ym)
     for h in range(2):
         for rel in range(1, 8):
             go(scatter(h, rel))
@@ -186,20 +196,24 @@
     vscr[...] = jnp.ones_like(vscr)
     for i in range(TP * FEAT // HD):
         at = slice(i * HD, (i + 1) * HD)
-        spread = jnp.where(eye, jnp.broadcast_to(gain_ref[:, at], (HD, HD)), 0.0)
+        spread = jnp.where(eye, jnp.broadcast_to(gain_ref[at].reshape(1, HD), (HD, HD)), 0.0)
         gcol[at, :] = jnp.broadcast_to(jnp.sum(spread, axis=1, keepdims=True), (HD, HD))
 
+    def scatter_waits(h):
+        for rel in range(1, 8):
+            scatter_wait(h, rel)
+
+    scatter_waits(0)
+    z_own(0)
     hid_wait(2, here + ym, None)
     hid_copy(4, here + ym, 0, here + yp)
     hid_wait(3, here + yp, None)
     hid_copy(5, here + yp, 1, here + ym)
-    for h in range(2):
-        for rel in range(1, 8):
-            scatter_wait(h, rel)
     hid_wait(0, there + y, 0)
     hid_copy(6, there + y, 0, here + yp)
     hid_copy(7, there + y, 0, here + ym)
-    z_own(0)
+    scatter_waits(1)
+    z_own(1)
     for i in range(1, TP):
         sq_wait(i)
     total = sq[0]
@@ -209,28 +223,26 @@
     for load in loads:
         load.wait()
     project(t, row_scale)
+    project(here + ym, row_scale)
+    hid_wait(6, there + ym, 0)
+    hid_copy(10, there + ym, 0, here + yp)
+    project(here + yp, row_scale)
     hid_wait(1, there + y, 1)
     hid_copy(8, there + y, 1, here + yp)
     hid_copy(9, there + y, 1, here + ym)
-    hid_wait(6, there + ym, 0)
-    hid_copy(10, there + ym, 0, here + yp)
-    project(here + ym, row_scale)
-    project(here + yp, row_scale)
-    hid_wait(9, there + yp, 1)
-    hid_copy(11, there + yp, 1, here + ym)
-    z_step(0, 0)
-    project(there + y, row_scale)
+    z_relay(0, 0, 1)
     hid_wait(4, here + yq, 0)
     hid_wait(5, here + yq, 1)
     project(here + yq, row_scale)
+    project(there + y, row_scale)
+    hid_wait(9, there + yp, 1)
+    hid_copy(11, there + yp, 1, here + ym)
     hid_wait(8, there + ym, 1)
     project(there + ym, row_scale)
     hid_wait(7, there + yp, 0)
     project(there + yp, row_scale)
     hid_wait(10, there + yq, 0)
     hid_wait(11, there + yq, 1)
-    z_step(0, 1)
-    z_own(1)
     project(there + yq, row_scale)
 
     cosine, sine = cos_ref[...], sin_ref[...]
@@ -266,8 +278,6 @@
         for n, rel in enumerate((2, 6, 4)):
             go(q_copy(h, s, n, 8 - rel, row_dev(slot_at(rel))))
         go(q_copy(h, s, 3, sib_rel(0), (sibling, t)))
-    z_step(0, 2)
-
     row_id = lax.broadcasted_iota(jnp.int32, (2 * ROWS, ROWS), 0) % ROWS
     col_id = lax.broadcasted_iota(jnp.int32, (2 * ROWS, ROWS), 1)
     causal = row_id >= col_id
@@ -358,16 +368,18 @@
             out = jnp.where(rows_live, num / den, 0.0).astype(BF)
             att_ref[r0 : r0 + HD, head * HD : (head + 1) * HD] = out
 
+    z_relay(0, 2)
+    z_relay(1, 0, 1)
     q_forward(0)
     q_rest(0)
-    attend_loop(0, 0, 3)
+    z_take(0)
+    attend_loop(0, 0, 4)
     q_forward(1)
-    z_step(1, 0)
-    attend_loop(0, 3, 8)
-    z_step(1, 1)
+    z_relay(1, 2)
+    attend_loop(0, 4, 8)
     q_rest(1)
     combine(0)
-    z_step(1, 2)
+    z_take(1)
     attend_loop(1, 0, 8)
     combine(1)
 
@@ -393,7 +405,6 @@
 
 
 def body(hidden, norm_gain, w_query, w_key, w_value, prefix_kv, group_of, block_owner, lengths):
-    gain = norm_gain.reshape(1, TP * FEAT)
     full_cos, signed_sin = rope_constants()
     smem = pl.BlockSpec(memory_space=pltpu.SMEM)
     vmem = pl.BlockSpec(memory_space=pltpu.VMEM)
@@ -434,11 +445,12 @@
             collective_id=1, has_side_effects=True, vmem_limit_bytes=56 * 2**20
         ),
     )(
-        group_of, block_owner, lengths, hidden.T, w_query, w_key, w_value, prefix_kv, gain,
+        group_of, block_owner, lengths, hidden.T, w_query, w_key, w_value, prefix_kv, norm_gain,
         jnp.asarray(full_cos), jnp.asarray(signed_sin),
     )
     return pl.pallas_call(
-        finish, out_shape=shapes, in_specs=[vmem] * 3, out_specs=(vmem, vmem, vmem), name="finish"
+        finish, out_shape=shapes, in_specs=[vmem] * 3, out_specs=(vmem, vmem, vmem), name="finish",
+        compiler_params=pltpu.CompilerParams(vmem_limit_bytes=4 * 2**20),
     )(*results)
 
 

time: 86.5 us -> 82.7 us (0.956)
  Pallas kernels: 84.4 us -> 79.1 us
  local copies, waits for them, and re-layouts: 1.35 us -> 2.75 us
    pallas_call x1, Pallas kernels: 82.5 us -> 78.3 us  [body(): pl.pallas_call(kernel, out_shape=shapes, in_specs=[smem] * 3 + [hbm] * 5...]
    unnamed x0 -> x6, local copies, waits for them, and re-layouts: none -> 2.75 us
    reshape x1 -> x0, local copies, waits for them, and re-layouts: 1.35 us -> none  [body(): gain = norm_gain.reshape(1, TP * FEAT)]
    pallas_call x1, Pallas kernels: 1.84 us -> 0.82 us  [body(): pl.pallas_call(finish, out_shape=shapes, in_specs=[vmem] * 3, out_specs=(...]
where the time goes in v3:
time: 82.7 us; the launch traced here: 82.6 us
  Pallas kernels  79.1 us (96%)
  local copies, waits for them, and re-layouts  2.75 us (3%)
    pallas_call x1, Pallas kernels, body(): pl.pallas_call(kernel, out_shape=shapes, in_specs=[smem] * 3 + [hbm] * 5...  78.3 us
    unnamed x6, local copies, waits for them, and re-layouts  2.75 us

profile of v3, /device:TPU:1, one launch (start us, length us, event | category | flops | bytes accessed | tf_op | source)
XLA Modules:
  0.0 82.6 jit_solution(7790805816729163368)
XLA Ops:
  0.6 78.3 %prefill.1 = (bf16[256,512]{1,0:T(8,128)(2,1)}, bf16[256,256]{1,0:T(8,128)(2,1)}, bf16[256,256]{1,0:T(8,128)(2,1)}) custom-call(s32[32]{0:T(128)} %group_ref.1, s32[4,8]{1,0:T(4,128)} %owner_ref.1, s32[32]{0:T(128)} %length_ref.1, bf16[576,256]{1,0:T(8,128)(2,1)} %bitcast.1, bf16[4608,512]{1,0:T(8,128)(2,1)} %wq.1, bf16[4608,256]{1,0:T(8,128)(2,1)} %wk.1, ...), custom_call_target="tpu_custom_call" | custom-call | tf_op jit(solution)/shard_map/prefill/pallas_call | solution.py:415
  79.0 0.0 copy-start
  79.0 0.9 %copy-done = bf16[256,512]{1,0:T(8,128)(2,1)S(1)} copy-done((bf16[256,512]{1,0:T(8,128)(2,1)S(1)}, bf16[256,512]{1,0:T(8,128)(2,1)}, u32[]{:S(2)}) %copy-start) | copy-done | bytes 262168
  79.9 0.0 copy-start.1
  79.9 0.9 %copy-done.1 = bf16[256,256]{1,0:T(8,128)(2,1)S(1)} copy-done((bf16[256,256]{1,0:T(8,128)(2,1)S(1)}, bf16[256,256]{1,0:T(8,128)(2,1)}, u32[]{:S(2)}) %copy-start.1) | copy-done | bytes 131096
  80.8 0.0 copy-start.2
  80.8 0.9 %copy-done.2 = bf16[256,256]{1,0:T(8,128)(2,1)S(1)} copy-done((bf16[256,256]{1,0:T(8,128)(2,1)S(1)}, bf16[256,256]{1,0:T(8,128)(2,1)}, u32[]{:S(2)}) %copy-start.2) | copy-done | bytes 131096
  81.7 0.8 finish.1
Async XLA Ops:
  79.0 1.0 %copy-start = (bf16[256,512]{1,0:T(8,128)(2,1)S(1)}, bf16[256,512]{1,0:T(8,128)(2,1)}, u32[]{:S(2)}) copy-start(bf16[256,512]{1,0:T(8,128)(2,1)} %get-tuple-element.6.att) | copy-start | bytes 786436
  79.9 0.9 %copy-start.1 = (bf16[256,256]{1,0:T(8,128)(2,1)S(1)}, bf16[256,256]{1,0:T(8,128)(2,1)}, u32[]{:S(2)}) copy-start(bf16[256,256]{1,0:T(8,128)(2,1)} %get-tuple-element.7.key) | copy-start | bytes 393220
  80.8 0.9 %copy-start.2 = (bf16[256,256]{1,0:T(8,128)(2,1)S(1)}, bf16[256,256]{1,0:T(8,128)(2,1)}, u32[]{:S(2)}) copy-start(bf16[256,256]{1,0:T(8,128)(2,1)} %get-tuple-element.8.val) | copy-start | bytes 393220

commit v4 on v3

--- a/solution.py
+++ b/solution.py
@@ -313,7 +313,10 @@
 
     def attend_loop(h, first, last):
         @pl.loop(first, last)
-        def _(i):
+        def _(n):
+            third, rest = n // 3, n % 3
+            shuffled = 1 - rest + (rest // 2) * 3 + 4 * third
+            i = (1 - third // 2) * shuffled + (third // 2) * (3 + 4 * rest)
             dx = (i + 1) % 4
             core = (1 - c) + (i // 4) * (2 * c - 1)
             slot = ((x + dx) % 4) * 2 + core
@@ -414,7 +417,7 @@
     shapes = tuple(jax.ShapeDtypeStruct((ROWS, n), BF) for n in (512, 256, 256))
     results = pl.pallas_call(
         kernel,
-        out_shape=shapes,
+        out_shape=tuple(pltpu.VMEM((ROWS, n), BF) for n in (512, 256, 256)),
         in_specs=[smem] * 3 + [hbm] * 5 + [vmem] * 3,
         out_specs=(vmem, vmem, vmem),
         scratch_shapes=[

time: 82.7 us -> 78.5 us (0.949)
  local copies, waits for them, and re-layouts: 2.75 us -> 0 us
  Pallas kernels: 79.1 us -> 77.8 us
    unnamed x6 -> x0, local copies, waits for them, and re-layouts: 2.75 us -> none
    pallas_call x1, Pallas kernels: 78.3 us -> 76.9 us  [body(): pl.pallas_call(kernel, out_shape=tuple((pltpu.VMEM((ROWS, n), BF) for n i...]
where the time goes in v4:
time: 78.5 us; the launch traced here: 78.4 us
  Pallas kernels  77.8 us (99%)
    pallas_call x1, Pallas kernels, body(): pl.pallas_call(kernel, out_shape=tuple((pltpu.VMEM((ROWS, n), BF) for n i...  76.9 us

profile of v4, /device:TPU:1, one launch (start us, length us, event | category | flops | bytes accessed | tf_op | source)
XLA Modules:
  0.0 78.4 jit_solution(3792335667674017553)
XLA Ops:
  0.6 76.9 %prefill.1 = (bf16[256,512]{1,0:T(8,128)(2,1)S(1)}, bf16[256,256]{1,0:T(8,128)(2,1)S(1)}, bf16[256,256]{1,0:T(8,128)(2,1)S(1)}) custom-call(s32[32]{0:T(128)} %group_ref.1, s32[4,8]{1,0:T(4,128)} %owner_ref.1, s32[32]{0:T(128)} %length_ref.1, bf16[576,256]{1,0:T(8,128)(2,1)} %bitcast.1, bf16[4608,512]{1,0:T(8,128)(2,1)} %wq.1, bf16[4608,256]{1,0:T(8,128)(2,1)} %wk.1, ...), custom_call_target="tpu_custom_call" | custom-call | tf_op jit(solution)/shard_map/prefill/pallas_call | solution.py:418
  77.6 0.8 %finish.1 = (bf16[256,512]{1,0:T(8,128)(2,1)}, bf16[256,256]{1,0:T(8,128)(2,1)}, bf16[256,256]{1,0:T(8,128)(2,1)}) custom-call(bf16[256,512]{1,0:T(8,128)(2,1)S(1)} %get-tuple-element.6.att, bf16[256,256]{1,0:T(8,128)(2,1)S(1)} %get-tuple-element.7.key, bf16[256,256]{1,0:T(8,128)(2,1)S(1)} %get-tuple-element.8.val), custom_call_target="tpu_custom_call" | custom-call | tf_op jit(solution)/shard_map/finish/pallas_call | solution.py:454

commit v5 on v4

--- a/solution.py
+++ b/solution.py
@@ -31,9 +31,9 @@
 
 
 def kernel(
-    group_ref, owner_ref, length_ref, hid, wq, wk, wv, kv, gain_ref, cos_ref, sin_ref,
+    group_ref, owner_ref, length_ref, hid, wq, wk, wv, kv, gain_hbm, cos_hbm, sin_hbm,
     att_ref, key_ref, val_ref,
-    hbuf, wbuf, kraw, kf32, kvs, kvb0, kvb1, qb0, qb1, ns0, ns1, nl0, nl1, ds0, ds1, dl0, dl1,
+    gain_ref, cos_ref, sin_ref, hbuf, wbuf, kraw, kf32, kvs, kvb0, kvb1, qb0, qb1, ns0, ns1, nl0, nl1, ds0, ds1, dl0, dl1,
     acc, sq, gcol, kscr, vscr, snum, sden,
     lsem, wsem, qss, qsr, hs, hr, cs, cr, zs, zr, qs, qr, rs, rr, es, er,
 ):
@@ -70,12 +70,17 @@
     own_hid.start()
     own_kv = pltpu.make_async_copy(kv, kraw, lsem.at[1])
     own_kv.start()
+    tables = [
+        pltpu.make_async_copy(gain_hbm, gain_ref, lsem.at[2]),
+        pltpu.make_async_copy(cos_hbm, cos_ref, lsem.at[3]),
+        pltpu.make_async_copy(sin_hbm, sin_ref, lsem.at[4]),
+    ]
     loads = [
         pltpu.make_async_copy(wq, wbuf.at[:, 0:512], wsem.at[0]),
         pltpu.make_async_copy(wk, wbuf.at[:, 512:768], wsem.at[1]),
         pltpu.make_async_copy(wv, wbuf.at[:, 768:1024], wsem.at[2]),
     ]
-    for load in loads:
+    for load in tables + loads:
         load.start()
 
     barrier = pltpu.get_barrier_semaphore()
@@ -193,6 +198,8 @@
             go(scatter(h, rel))
 
     acc[...] = jnp.zeros_like(acc)
+    for load in tables:
+        load.wait()
     vscr[...] = jnp.ones_like(vscr)
     for i in range(TP * FEAT // HD):
         at = slice(i * HD, (i + 1) * HD)
@@ -418,9 +425,12 @@
     results = pl.pallas_call(
         kernel,
         out_shape=tuple(pltpu.VMEM((ROWS, n), BF) for n in (512, 256, 256)),
-        in_specs=[smem] * 3 + [hbm] * 5 + [vmem] * 3,
+        in_specs=[smem] * 3 + [hbm] * 8,
         out_specs=(vmem, vmem, vmem),
         scratch_shapes=[
+            pltpu.VMEM((TP * FEAT,), F32),
+            pltpu.VMEM((ROWS, HD), F32),
+            pltpu.VMEM((ROWS, HD), F32),
             pltpu.VMEM((TP, FEAT, ROWS), BF),
             pltpu.VMEM((TP * FEAT, 1024), BF),
             pltpu.VMEM((512, 2, 256), BF),
@@ -439,7 +449,7 @@
             pltpu.VMEM((512, 2 * HD), BF),
             pltpu.VMEM((2, 512, HD), F32),
             pltpu.VMEM((2, 512, HD), F32),
-            dma((2,)), dma((3,)), dma((8,)), dma((8,)), dma((12,)), dma((12,)),
+            dma((5,)), dma((3,)), dma((8,)), dma((8,)), dma((12,)), dma((12,)),
             dma((2, 8)), dma((2, 8)), dma((2, 5)), dma((2, 3)),
             dma((2, 8)), dma((2, 8)), dma((2, 8)), dma((2, 8)), dma((2, 8)), dma((2, 8)),
         ],

time: 78.5 us -> 78.3 us (level)
  no operation moved by 1% of the time
where the time goes in v5:
time: 78.3 us; the launch traced here: 78.2 us
  Pallas kernels  77.5 us (99%)
    pallas_call x1, Pallas kernels, body(): pl.pallas_call(kernel, out_shape=tuple((pltpu.VMEM((ROWS, n), BF) for n i...  76.7 us

profile of v5, /device:TPU:1, one launch (start us, length us, event | category | flops | bytes accessed | tf_op | source)
XLA Modules:
  0.0 78.2 jit_solution(9845382721071463491)
XLA Ops:
  0.6 76.7 %prefill.1 = (bf16[256,512]{1,0:T(8,128)(2,1)S(1)}, bf16[256,256]{1,0:T(8,128)(2,1)S(1)}, bf16[256,256]{1,0:T(8,128)(2,1)S(1)}) custom-call(s32[32]{0:T(128)} %group_ref.1, s32[4,8]{1,0:T(4,128)} %owner_ref.1, s32[32]{0:T(128)} %length_ref.1, bf16[576,256]{1,0:T(8,128)(2,1)} %bitcast.1, bf16[4608,512]{1,0:T(8,128)(2,1)} %wq.1, bf16[4608,256]{1,0:T(8,128)(2,1)} %wk.1, ...), custom_call_target="tpu_custom_call" | custom-call | tf_op jit(solution)/shard_map/prefill/pallas_call | solution.py:425
  77.3 0.8 %finish.1 = (bf16[256,512]{1,0:T(8,128)(2,1)}, bf16[256,256]{1,0:T(8,128)(2,1)}, bf16[256,256]{1,0:T(8,128)(2,1)}) custom-call(bf16[256,512]{1,0:T(8,128)(2,1)S(1)} %get-tuple-element.6.att, bf16[256,256]{1,0:T(8,128)(2,1)S(1)} %get-tuple-element.7.key, bf16[256,256]{1,0:T(8,128)(2,1)S(1)} %get-tuple-element.8.val), custom_call_target="tpu_custom_call" | custom-call | tf_op jit(solution)/shard_map/finish/pallas_call | solution.py:464
